TPU v7x, 128 devices: a whole 4x4x4 slice. The times are simulated.
128 devices in a mesh: slab: 16 (over y, x_lo, core), head: 8 (over z, x_hi).
Axes of the slice: x: 4 (x_hi: 2, x_lo: 2; x = x_hi * 2 + x_lo), y: 4, z: 4, core: 2. Of those that a mesh axis runs over, the one named last changes fastest.
Arguments:
- hidden_states: bfloat16 [6144, 6144], P(('slab', 'head')), may hold values from -36 to 36
- qkv_weight: bfloat16 [3, 6144, 3072], P(None, None, 'head'), may hold values from -0.078125 to 0.078125
- out_grad: bfloat16 [6144, 3072], P('slab', 'head'), may hold values from -6 to 6
- tile_frame: int32 [48], replicated, may hold values from 0 to 2, as said below
- frame_band: int32 [24], P('head'), may hold values from 0 to 2
Outputs:
- attn_out: bfloat16 [6144, 3072], P('slab', 'head')
- grad_hidden: bfloat16 [6144, 6144], P(('slab', 'head'))
Inputs may be any that keep to these rules, and one draw needn't show every extreme that they name: `tile_frame`: the tiles of one frame are consecutive; tile 0 lies in frame 0, each tile lies in the frame of the tile before it or in the next one, and the last tile lies in frame 2.
All inputs are finite; a program needn't handle non-finite values.
Results may differ from a plain program's by a relative error of at most 0.03.
The roundings to bfloat16 on the way count: a program that leaves them out, or rounds other values in their place, can miss the bound.
Values may be sent and summed in bfloat16 or wider, within the bound.
No kernel may reach another device: no remote copies, remote signals or barrier semaphores. Data moves between devices by JAX's collectives and lax.ppermute only.
A program may use at most 192 MiB of HBM per device.

v0:
```python
import math

import jax
import jax.numpy as jnp
from jax import lax
from jax.sharding import PartitionSpec as P

TILE = 128


def body(hidden_states, qkv_weight, out_grad, tile_frame, frame_band):
    local_heads = frame_band.shape[0]
    qkv_width = qkv_weight.shape[2]
    head_dim = qkv_width // local_heads
    factor = 1.0 / math.sqrt(head_dim)
    stacked = jnp.einsum(
        "rd,cde->cre",
        lax.all_gather(hidden_states, "head", axis=0, tiled=True),
        qkv_weight,
        preferred_element_type=jnp.float32,
    ).astype(jnp.bfloat16)
    row_count = stacked.shape[1]
    slab_count = lax.axis_size("slab")
    tokens = row_count * slab_count
    block_rows = 2 * row_count
    frames = jnp.repeat(tile_frame, TILE)
    own_start = lax.axis_index("slab") * row_count
    query_frames = lax.dynamic_slice_in_dim(frames, own_start, row_count)
    queries = stacked[0].reshape(row_count, local_heads, head_dim)
    keys_flat = stacked[1]
    values_flat = stacked[2]

    def masked_scores(query_part, key_part, query_place, key_place):
        scores = (
            jnp.einsum("qhd,khd->hqk", query_part, key_part, preferred_element_type=jnp.float32)
            * factor
        )
        distance = jnp.abs(query_place[:, None] - key_place[None, :])
        inside = distance[None, :, :] <= frame_band[:, None, None]
        return (jnp.where(inside, scores, -1e30), inside)

    def attend(running_state, key_piece, value_piece, start):
        running, weight_sum, accumulated = running_state
        piece_rows = key_piece.shape[0]
        key_place = lax.dynamic_slice_in_dim(frames, start, piece_rows)
        key_heads = key_piece.reshape(piece_rows, local_heads, head_dim)
        value_heads = value_piece.reshape(piece_rows, local_heads, head_dim)
        masked, inside = masked_scores(queries, key_heads, query_frames, key_place)
        new_peak = jnp.maximum(running, jnp.max(masked, axis=2))
        shrink = jnp.exp(running - new_peak)
        weights = jnp.where(inside, jnp.exp(masked - new_peak[:, :, None]), 0.0)
        weight_sum = weight_sum * shrink + jnp.sum(weights, axis=2)
        update = jnp.einsum(
            "hqk,khd->qhd",
            weights.astype(jnp.bfloat16),
            value_heads,
            preferred_element_type=jnp.float32,
        )
        accumulated = accumulated * shrink.T[:, :, None] + update
        return (new_peak, weight_sum, accumulated)

    initial = (
        jnp.full((local_heads, row_count), -1e30, jnp.float32),
        jnp.zeros((local_heads, row_count), jnp.float32),
        jnp.zeros((row_count, local_heads, head_dim), jnp.float32),
    )

    def block_grads(
        query_part, grad_part, lse_part, delta_part, query_place, key_part, value_part, key_place
    ):
        masked, inside = masked_scores(query_part, key_part, query_place, key_place)
        probabilities = jnp.where(inside, jnp.exp(masked - lse_part[:, :, None]), 0.0)
        value_grad = jnp.einsum(
            "hqk,qhd->khd",
            probabilities.astype(jnp.bfloat16),
            grad_part,
            preferred_element_type=jnp.float32,
        )
        grad_probs = jnp.einsum(
            "qhd,khd->hqk", grad_part, value_part, preferred_element_type=jnp.float32
        )
        grad_scores = (probabilities * (grad_probs - delta_part[:, :, None])).astype(jnp.bfloat16)
        query_grad = (
            jnp.einsum("hqk,khd->qhd", grad_scores, key_part, preferred_element_type=jnp.float32)
            * factor
        )
        key_grad = (
            jnp.einsum("hqk,qhd->khd", grad_scores, query_part, preferred_element_type=jnp.float32)
            * factor
        )
        return (query_grad, key_grad, value_grad)

    grad_out = out_grad.reshape(row_count, local_heads, head_dim)
    key_all, value_all = (
        lax.all_gather(keys_flat, "slab", axis=0, tiled=True),
        lax.all_gather(values_flat, "slab", axis=0, tiled=True),
    )

    def forward_block(block_index, running_state):
        start = block_index * block_rows
        key_piece = lax.dynamic_slice_in_dim(key_all, start, block_rows)
        value_piece = lax.dynamic_slice_in_dim(value_all, start, block_rows)
        return attend(running_state, key_piece, value_piece, start)

    running, weight_sum, accumulated = lax.fori_loop(0, slab_count // 2, forward_block, initial)
    output = (accumulated / weight_sum.T[:, :, None]).astype(jnp.bfloat16)
    attn_out = output.reshape(row_count, qkv_width)
    log_total = running + jnp.log(weight_sum)
    row_delta = jnp.sum(grad_out.astype(jnp.float32) * output.astype(jnp.float32), axis=2).T

    def backward_block(block_index, state_pair):
        query_acc, key_terms = state_pair
        start = block_index * block_rows
        key_part = lax.dynamic_slice_in_dim(key_all, start, block_rows).reshape(
            block_rows, local_heads, head_dim
        )
        value_part = lax.dynamic_slice_in_dim(value_all, start, block_rows).reshape(
            block_rows, local_heads, head_dim
        )
        key_place = lax.dynamic_slice_in_dim(frames, start, block_rows)
        part_query, part_key, part_value = block_grads(
            queries, grad_out, log_total, row_delta, query_frames, key_part, value_part, key_place
        )
        key_block = jnp.concatenate(
            [part_key.reshape(block_rows, qkv_width), part_value.reshape(block_rows, qkv_width)],
            axis=1,
        )
        key_terms = lax.dynamic_update_slice_in_dim(key_terms, key_block, start, 0)
        return (query_acc + part_query, key_terms)

    start_pair = (
        jnp.zeros((row_count, local_heads, head_dim), jnp.float32),
        jnp.zeros((tokens, 2 * qkv_width), jnp.float32),
    )
    query_acc, key_terms = lax.fori_loop(0, slab_count // 2, backward_block, start_pair)
    summed = lax.psum_scatter(
        key_terms.astype(jnp.bfloat16), "slab", scatter_dimension=0, tiled=True
    ).astype(jnp.float32)
    query_final = query_acc.reshape(row_count, qkv_width).astype(jnp.bfloat16)
    key_final = summed[:, :qkv_width].astype(jnp.bfloat16)
    value_final = summed[:, qkv_width:].astype(jnp.bfloat16)
    all_grads = jnp.stack([query_final, key_final, value_final])
    grad_hidden = lax.psum_scatter(
        jnp.einsum("cre,cde->rd", all_grads, qkv_weight, preferred_element_type=jnp.float32).astype(
            jnp.bfloat16
        ),
        "head",
        scatter_dimension=0,
        tiled=True,
    )
    return (attn_out, grad_hidden)


def solution(mesh):
    placed = (P(("slab", "head"), None), P(None, None, "head"), P("slab", "head"), P(), P("head"))
    return jax.shard_map(
        body,
        mesh=mesh,
        in_specs=placed,
        out_specs=(P("slab", "head"), P(("slab", "head"), None)),
        check_vma=False,
    )
```

profile of v0, /device:TPU:0, one launch (start us, length us, event | category | flops | bytes accessed | tf_op | source)
XLA Modules:
  0.0 526.1 jit_solution(16420702500654508604)
XLA Ops:
  8.0 80.8 %all-gather.6.cloned.1.call-done = bf16[384,6144]{1,0:T(8,128)(2,1)} async-done(((bf16[48,6144]{1,0:T(8,128)(2,1)}), bf16[384,6144]{1,0:T(8,128)(2,1)}) %all-gather.6.cloned.1.call-update) | async-done | bytes 4718608 | tf_op jit(solution)/shard_map/all_gather | solution.py:18
  88.8 11.6 %fusion.32 = bf16[3,384,384]{1,2,0:T(8,128)(2,1)S(1)} fusion(bf16[3,6144,384]{2,1,0:T(8,128)(2,1)} %param.10, bf16[384,6144]{1,0:T(8,128)(2,1)} %all-gather.6.cloned.1.call-done), kind=kOutput, calls=%fused_computation.44 | convolution fusion | flops 5436260352 | bytes 19759104 | tf_op jit(solution)/shard_map/rd,cde->cre/dot_general | solution.py:16
  104.2 33.6 %all-gather.10.cloned.1.call-done = bf16[1,6144,384]{1,2,0:T(8,128)(2,1)} async-done(((bf16[1,384,384]{1,2,0:T(8,128)(2,1)}), bf16[1,6144,384]{1,2,0:T(8,128)(2,1)}) %all-gather.10.cloned.1.call-update) | async-done | bytes 4718608 | tf_op jit(solution)/shard_map/all_gather | solution.py:96
  137.8 41.0 %all-gather.8.cloned.1.call-done = bf16[1,6144,384]{1,2,0:T(8,128)(2,1)} async-done(((bf16[1,384,384]{1,2,0:T(8,128)(2,1)}), bf16[1,6144,384]{1,2,0:T(8,128)(2,1)}) %all-gather.8.cloned.1.call-update) | async-done | bytes 4718608 | tf_op jit(solution)/shard_map/all_gather | solution.py:95
  178.9 45.7 %while.34 = (s32[]{:T(128)}, f32[3,384]{1,0:T(4,128)S(1)}, f32[3,384]{1,0:T(4,128)S(1)}, f32[384,3,128]{0,2,1:T(8,128)S(1)}, s32[384]{0:T(512)S(1)}, /*index=5*/...) while((s32[]{:T(128)}, f32[3,384]{1,0:T(4,128)S(1)}, ...), condition=%wide.region_3.4_spmd.clone, body=%wide.region_0.3_spmd.clone.sunk | while | flops 468179712 | bytes 20433652 | solution.py:105
  179.9 1.3 constant_dynamic-slice_fusion.6
  182.3 1.3 fusion.88
  185.6 1.3 constant_dynamic-slice_fusion.6
  186.9 1.1 fusion.84
  188.0 1.3 fusion.88
  191.3 1.3 constant_dynamic-slice_fusion.6
  192.6 1.1 fusion.84
  193.7 1.3 fusion.88
  197.0 1.3 constant_dynamic-slice_fusion.6
  199.4 1.3 fusion.88
  202.7 1.3 constant_dynamic-slice_fusion.6
  205.1 1.3 fusion.88
  208.5 1.3 constant_dynamic-slice_fusion.6
  209.8 1.1 fusion.84
  210.9 1.3 fusion.88
  214.2 1.3 constant_dynamic-slice_fusion.6
  215.5 1.1 fusion.84
  216.6 1.3 fusion.88
  219.9 1.3 constant_dynamic-slice_fusion.6
  222.3 1.3 fusion.88
  225.2 1.4 multiply_reduce_fusion
  226.6 4.3 broadcast_in_dim.81.clone
  230.8 81.4 %while.35 = (s32[]{:T(128)}, f32[384,3,128]{0,2,1:T(8,128)S(1)}, bf16[6144,768]{1,0:T(8,128)(2,1)}, bf16[6144,384]{0,1:T(8,128)(2,1)}, s32[384]{0:T(512)S(1)}, /...) while((s32[]{:T(128)}, f32[384,3,128]{0,2,1:T(8,128)S(1)}, ...), condition=%wide.region_6.7_spmd.clone, body=%wide.region_5.6_spmd.clone.sunk | while | flops 1148829696 | bytes 34234616 | solution.py:135
  231.8 1.3 constant_dynamic-slice_fusion.7
  233.8 1.8 fusion.102
  235.7 2.3 fusion.100
  239.9 1.1 constant_dynamic-update-slice_fusion.2
  242.0 1.3 constant_dynamic-slice_fusion.7
  244.0 1.8 fusion.102
  245.8 2.3 fusion.100
  250.0 1.1 constant_dynamic-update-slice_fusion.2
  252.1 1.3 constant_dynamic-slice_fusion.7
  254.2 1.8 fusion.102
  256.0 2.3 fusion.100
  260.2 1.1 constant_dynamic-update-slice_fusion.2
  262.3 1.3 constant_dynamic-slice_fusion.7
  264.3 1.8 fusion.102
  266.1 2.3 fusion.100
  270.3 1.1 constant_dynamic-update-slice_fusion.2
  272.5 1.3 constant_dynamic-slice_fusion.7
  274.5 1.8 fusion.102
  276.3 2.3 fusion.100
  280.5 1.1 constant_dynamic-update-slice_fusion.2
  282.6 1.3 constant_dynamic-slice_fusion.7
  284.6 1.8 fusion.102
  286.5 2.3 fusion.100
  290.7 1.1 constant_dynamic-update-slice_fusion.2
  292.8 1.3 constant_dynamic-slice_fusion.7
  294.8 1.8 fusion.102
  296.6 2.3 fusion.100
  300.9 1.1 constant_dynamic-update-slice_fusion.2
  303.0 1.3 constant_dynamic-slice_fusion.7
  305.0 1.8 fusion.102
  306.8 2.3 fusion.100
  311.0 1.2 constant_dynamic-update-slice_fusion.2
  312.8 108.1 %reduce-scatter.3.cloned.1.call-done = bf16[384,768]{1,0:T(8,128)(2,1)} async-done(((bf16[6144,768]{1,0:T(8,128)(2,1)}), bf16[384,768]{1,0:T(8,128)(2,1)}) %reduce-scatter.3.cloned.1.call-update) | async-done | bytes 589840 | tf_op jit(solution)/shard_map/reduce_scatter | solution.py:136
  420.8 1.1 slice_bitcast_fusion.1
  421.9 11.0 %bitcast_convert_fusion = bf16[384,6144]{1,0:T(8,128)(2,1)} fusion(bf16[3,6144,384]{2,1,0:T(8,128)(2,1)} %param.10, bf16[1,384,384]{2,1,0:T(8,128)(2,1)S(1)} %get-tuple-element.542, bf16[1,384,384]{2,1,0:T(8,128)(2,1)S(1)} %get-tuple-element.541, bf16[1,384,384]{2,1,0:T(8,128)(2,1)S(1)} %copy.36), kind=kOutput, calls=%fused_computation.40 | convolution fusion | flops 5439062016 | bytes 19759104 | tf_op jit(solution)/shard_map/cre,cde->rd/dot_general | solution.py:144
  434.8 84.8 %reduce-scatter.5.cloned.1.call-done = bf16[48,6144]{1,0:T(8,128)(2,1)} async-done(((bf16[384,6144]{1,0:T(8,128)(2,1)}), bf16[48,6144]{1,0:T(8,128)(2,1)}) %reduce-scatter.5.cloned.1.call-update) | async-done | bytes 589840 | tf_op jit(solution)/shard_map/reduce_scatter | solution.py:143
  (139 shorter events, 56.6 us)
Async XLA Ops:
  7.2 95.4 %copy-start = (s32[48]{0:T(128)S(1)}, s32[48]{0:T(128)}, u32[]{:S(2)}) copy-start(s32[48]{0:T(128)} %param.12) | copy-start | bytes 580
  7.2 81.6 %all-gather.6.cloned.1.call-start = ((), (), s32[]{:S(2)}) async-start(), calls=%async_computation.2 | async-start | bytes 5308416 | tf_op jit(solution)/shard_map/all_gather | solution.py:18
  7.9 94.4 %copy-start.2 = (bf16[384,384]{1,0:T(8,128)(2,1)S(1)}, bf16[384,384]{1,0:T(8,128)(2,1)}, u32[]{:S(2)}) copy-start(bf16[384,384]{1,0:T(8,128)(2,1)} %param.11) | copy-start | bytes 884740
  7.9 129.9 %all-gather.10.cloned.1.call-start = ((), (), s32[]{:S(2)}) async-start(), calls=%async_computation.6 | async-start | bytes 5013504 | tf_op jit(solution)/shard_map/all_gather | solution.py:96
  100.3 78.5 %copy-start.3 = (s32[3]{0:T(128)S(1)}, s32[3]{0:T(128)}, u32[]{:S(2)}) copy-start(s32[3]{0:T(128)} %param.13) | copy-start | bytes 40
  101.3 77.6 %all-gather.8.cloned.1.call-start = ((), (), s32[]{:S(2)}) async-start(), calls=%async_computation.5 | async-start | bytes 5013504 | tf_op jit(solution)/shard_map/all_gather | solution.py:95
  102.0 318.8 %reduce-scatter.3.cloned.1.call-start = ((), (), s32[]{:S(2)}) async-start(), calls=%async_computation.3 | async-start | bytes 10027008 | tf_op jit(solution)/shard_map/reduce_scatter | solution.py:136
  312.2 207.3 %reduce-scatter.5.cloned.1.call-start = ((), (), s32[]{:S(2)}) async-start(), calls=%async_computation.4 | async-start | bytes 5308416 | tf_op jit(solution)/shard_map/reduce_scatter | solution.py:143
  432.9 1.0 copy-start.1
Sparse Core Ops, SparseCore 0:
  10.3 78.4 all-gather.5
  101.4 36.3 all-gather.9
  140.1 38.7 all-gather.7
  312.4 108.4 reduce-scatter.2
  433.1 86.4 reduce-scatter.4
where the time goes:
time: 529 us; the launch traced here: 526 us
  waiting for transfers between devices  350 us (66%)
  matrix products  88.6 us (17%)
  local copies, waits for them, and re-layouts  58 us (11%)
  other arithmetic  14.4 us (3%)
  between operations  13.9 us (3%)
    reduce_scatter x1, waiting for transfers between devices, body(): lax.psum_scatter(key_terms.astype(jnp.bfloat16), 'slab', scatter_dimensio...  108 us
    reduce_scatter x1, waiting for transfers between devices, body(): lax.psum_scatter(jnp.einsum('cre,cde->rd', all_grads, qkv_weight, preferr...  84.8 us
    all_gather x1, waiting for transfers between devices, body(): lax.all_gather(hidden_states, 'head', axis=0, tiled=True)  80.8 us
    all_gather x1, waiting for transfers between devices, body(): lax.all_gather(keys_flat, 'slab', axis=0, tiled=True)  41 us
    all_gather x1, waiting for transfers between devices, body(): lax.all_gather(values_flat, 'slab', axis=0, tiled=True)  33.6 us
    dot_general x8, matrix products, block_grads(): jnp.einsum('qhd,khd->hqk', grad_part, value_part, preferred_element_type=...  18.2 us
    dot_general x8, matrix products, block_grads(): jnp.einsum('hqk,qhd->khd', probabilities.astype(jnp.bfloat16), grad_part,...  14.4 us
    dynamic_update_slice x16, local copies, waits for them, and re-layouts, backward_block(): key_terms = lax.dynamic_update_slice_in_dim(key_terms, key_block, start, 0)  14.2 us
  transfers between devices with their start and end apart: 5, of which 5 were waited for; matrix products, arithmetic and copies ran while one was open for 1% of the time, Pallas kernels for 0%

commit v1 on v0

v1 whole, which is shorter than its diff:
```python
import functools
import math

import jax
import jax.numpy as jnp
from jax import lax
from jax.experimental import pallas as pl
from jax.experimental.pallas import tpu as pltpu
from jax.sharding import PartitionSpec as P

TILE = 128
BF = jnp.bfloat16
F32 = jnp.float32
NT_DIMS = (((1,), (1,)), ((), ()))
FAR = 1e30
FROM = ((0, 1, 2, 3), (2, 0, 3, 1), (1, 3, 0, 2), (3, 2, 1, 0))
STEPS = (0, -1, 1, 2)


def params():
    return pltpu.CompilerParams(vmem_limit_bytes=60 * 1024 * 1024)


def dot(a, b):
    return jnp.dot(a, b, preferred_element_type=F32)


def dot_nt(a, b):
    return lax.dot_general(a, b, NT_DIMS, preferred_element_type=F32)


def project_kernel(last, place, *refs):
    blocks, (w_ref, acc_in), outs, (rows, acc) = refs[:8], refs[8:10], refs[10:-2], refs[-2:]
    step = pl.program_id(0)

    @pl.when(step == 0)
    def _():
        if acc_in is None:
            acc[...] = jnp.zeros_like(acc)
        else:
            acc[...] = acc_in[...]

    height = blocks[0].shape[0]
    for i, block in enumerate(blocks):
        rows[pl.ds(pl.multiple_of(place[i] * height, 16), height), :] = block[...]
    x = rows[...]
    for c in range(3):
        acc[c] += dot(x, w_ref[c])

    @pl.when(step == pl.num_programs(0) - 1)
    def _():
        if last:
            q_ref, kv_ref = outs
            width = acc.shape[2]
            q_ref[...] = acc[0].astype(BF)
            kv_ref[:, :width] = acc[1].astype(BF)
            kv_ref[:, width:] = acc[2].astype(BF)
        else:
            outs[0][...] = acc[...]


def project(place, blocks, weight, half, acc=None, chunk=512):
    height, columns = blocks[0].shape
    width = weight.shape[2]
    total = 8 * height
    steps = columns // chunk
    block_spec = pl.BlockSpec((height, chunk), lambda k, place: (0, k))
    w_spec = pl.BlockSpec((3, chunk, width), lambda k, place: (0, k + half * steps, 0))
    acc_shape = jax.ShapeDtypeStruct((3, total, width), F32)
    whole = pl.BlockSpec((3, total, width), lambda k, place: (0, 0, 0))
    if acc is None:
        body = lambda place, *refs: project_kernel(False, place, *refs[:9], None, *refs[9:])
        ins, extra, out_shape, out_specs = [], [], acc_shape, whole
    else:
        body = functools.partial(project_kernel, True)
        ins, extra = [acc], [whole]
        out_shape = (
            jax.ShapeDtypeStruct((total, width), BF),
            jax.ShapeDtypeStruct((total, 2 * width), BF),
        )
        out_specs = (
            pl.BlockSpec((total, width), lambda k, place: (0, 0)),
            pl.BlockSpec((total, 2 * width), lambda k, place: (0, 0)),
        )
    return pl.pallas_call(
        body,
        out_shape=out_shape,
        grid_spec=pltpu.PrefetchScalarGridSpec(
            num_scalar_prefetch=1,
            grid=(steps,),
            in_specs=[block_spec] * 8 + [w_spec] + extra,
            out_specs=out_specs,
            scratch_shapes=[pltpu.VMEM((total, chunk), BF), pltpu.VMEM((3, total, width), F32)],
        ),
        compiler_params=params(),
        name="project",
    )(place, *blocks, weight, *ins)


def forward_kernel(scale2, q0, q1, q2, q3, g0, g1, g2, g3, kv0, kv1, kv2, kv3, bias, ot, stat, qs, gt, kv, vt):
    size, width = q0.shape
    heads = width // TILE
    for b, (q, g, k) in enumerate(((q0, g0, kv0), (q1, g1, kv1), (q2, g2, kv2), (q3, g3, kv3))):
        qs[b] = q[...]
        kv[b * size : (b + 1) * size, :] = k[:, :width]
        for h in range(heads):
            at = slice(h * TILE, (h + 1) * TILE)
            gt[b, h] = g[:, at].T
            vt[h, :, b * size : (b + 1) * size] = k[:, width + h * TILE : width + (h + 1) * TILE].T
    tiles = kv.shape[0] // TILE

    def step(b, carry):
        for h in range(heads):
            at = slice(h * TILE, (h + 1) * TILE)
            s = dot_nt(kv[:, at], qs[b, :, at])
            away = bias[b, h]
            peak = jnp.full((1, size), -FAR, F32)
            for t in range(tiles):
                top = jnp.max(s[t * TILE : (t + 1) * TILE], axis=0, keepdims=True) * scale2
                peak = jnp.maximum(peak, top + away[t : t + 1])
            total = jnp.zeros((1, size), F32)
            parts = []
            for t in range(tiles):
                base = jnp.where(away[t : t + 1] < 0, FAR, peak)
                p = jnp.exp2(s[t * TILE : (t + 1) * TILE] * scale2 - base)
                total = total + jnp.sum(p, axis=0, keepdims=True)
                parts.append(p.astype(BF))
            o = dot(vt[h], jnp.concatenate(parts, axis=0))
            stat[b, 3 * h : 3 * h + 1, :] = peak
            stat[b, 3 * h + 1 : 3 * h + 2, :] = total
            stat[b, 3 * h + 2 : 3 * h + 3, :] = jnp.sum(o * gt[b, h].astype(F32), axis=0, keepdims=True)
            ot[b, h] = (o * jnp.where(total > 0, 1.0 / total, 0.0)).astype(BF)
        return carry

    lax.fori_loop(0, 4, step, 0)


def forward(scale2, queries, grads, pairs, bias):
    size, width = queries[0].shape
    heads = width // TILE
    return pl.pallas_call(
        functools.partial(forward_kernel, scale2),
        out_shape=(
            jax.ShapeDtypeStruct((4, heads, TILE, size), BF),
            jax.ShapeDtypeStruct((4, 3 * heads, size), F32),
        ),
        scratch_shapes=[
            pltpu.VMEM((4, size, width), BF),
            pltpu.VMEM((4, heads, TILE, size), BF),
            pltpu.VMEM((4 * size, width), BF),
            pltpu.VMEM((heads, TILE, 4 * size), BF),
        ],
        compiler_params=params(),
        name="forward",
    )(*queries, *grads, *pairs, bias)


def totals_kernel(s0, s1, s2, s3, lse_ref, delta_ref):
    heads = lse_ref.shape[1]
    sources = (s0, s1, s2, s3)
    for p in range(4):
        for h in range(heads):
            rows = [
                [s[FROM[j][p], 3 * h + i : 3 * h + i + 1, :] for i in range(3)]
                for j, s in enumerate(sources)
            ]
            peak = functools.reduce(jnp.maximum, [r[0] for r in rows])
            shrink = [jnp.exp2(r[0] - peak) for r in rows]
            total = sum(r[1] * f for r, f in zip(rows, shrink))
            lse_ref[p, h : h + 1, :] = peak + jnp.log2(total)
            delta_ref[p, h : h + 1, :] = sum(r[2] * f for r, f in zip(rows, shrink)) / total


def totals(stats):
    _, rows, size = stats[0].shape
    shape = jax.ShapeDtypeStruct((4, rows // 3, size), F32)
    return pl.pallas_call(totals_kernel, out_shape=(shape, shape), compiler_params=params(), name="totals")(*stats)


def merge_kernel(o0, o1, o2, o3, s0, s1, s2, s3, out):
    heads = o0.shape[0]
    for h in range(heads):
        rows = [
            [s[FROM[j][0], 3 * h + i : 3 * h + i + 1, :] for i in range(2)]
            for j, s in enumerate((s0, s1, s2, s3))
        ]
        peak = functools.reduce(jnp.maximum, [r[0] for r in rows])
        shares = [r[1] * jnp.exp2(r[0] - peak) for r in rows]
        whole = sum(shares)
        o = sum(x[h].astype(F32) * (share / whole) for x, share in zip((o0, o1, o2, o3), shares))
        out[:, h * TILE : (h + 1) * TILE] = o.T.astype(BF)


def merge(outs, stats):
    heads, _, size = outs[0].shape
    return pl.pallas_call(
        merge_kernel,
        out_shape=jax.ShapeDtypeStruct((size, heads * TILE), BF),
        compiler_params=params(),
        name="merge",
    )(*outs, *stats)


def backward_kernel(scale2, factor, first, *refs):
    q_refs, g_refs, (kv_a, kv_b, lse, delta, bias) = refs[:4], refs[4:8], refs[8:13]
    rest = refs[13:]
    if first:
        dq_in, (dkv_a, dkv_b, dq_out) = None, rest[:3]
    else:
        dq_in, (dkv_a, dkv_b, dq_out) = rest[0], rest[1:4]
    qs, gs, ks, vs, kt, dk, dv = rest[-7:]
    size, width = q_refs[0].shape
    heads = width // TILE
    for b in range(4):
        qs[b] = q_refs[b][...]
        gs[b] = g_refs[b][...]
    for i, k in enumerate((kv_a, kv_b)):
        ks[i * size : (i + 1) * size, :] = k[:, :width]
        vs[i * size : (i + 1) * size, :] = k[:, width:]
        for h in range(heads):
            kt[h, :, i * size : (i + 1) * size] = k[:, h * TILE : (h + 1) * TILE].T
    dk[...] = jnp.zeros_like(dk)
    dv[...] = jnp.zeros_like(dv)
    tiles = 2 * size // TILE

    def step(b, carry):
        for h in range(heads):
            at = slice(h * TILE, (h + 1) * TILE)
            q, g = qs[b, :, at], gs[b, :, at]
            s = dot_nt(ks[:, at], q)
            dp = dot_nt(vs[:, at], g)
            away, top, shift = bias[b, h], lse[b, h : h + 1], delta[b, h : h + 1]
            probs, grads = [], []
            for t in range(tiles):
                rows = slice(t * TILE, (t + 1) * TILE)
                base = jnp.where(away[t : t + 1] < 0, FAR, top)
                p = jnp.exp2(s[rows] * scale2 - base)
                probs.append(p.astype(BF))
                grads.append((p * (dp[rows] - shift)).astype(BF))
            p = jnp.concatenate(probs, axis=0)
            ds = jnp.concatenate(grads, axis=0)
            dv[:, at] += dot(p, g)
            dk[:, at] += dot(ds, q)
            dq = dot(kt[h], ds)
            if first:
                dq_out[b, h] = dq
            else:
                dq_out[b, :, at] = ((dq_in[b, h] + dq) * factor).T.astype(BF)
        return carry

    lax.fori_loop(0, 4, step, 0)
    for i, out in enumerate((dkv_a, dkv_b)):
        rows = slice(i * size, (i + 1) * size)
        out[:, :width] = (dk[rows] * factor).astype(BF)
        out[:, width:] = dv[rows].astype(BF)


def backward(scale2, factor, queries, grads, pairs, lse, delta, bias, dq=None):
    size, width = queries[0].shape
    heads = width // TILE
    pair = jax.ShapeDtypeStruct((size, 2 * width), BF)
    if dq is None:
        dq_shape = jax.ShapeDtypeStruct((4, heads, TILE, size), F32)
    else:
        dq_shape = jax.ShapeDtypeStruct((4, size, width), BF)
    return pl.pallas_call(
        functools.partial(backward_kernel, scale2, factor, dq is None),
        out_shape=(pair, pair, dq_shape),
        scratch_shapes=[
            pltpu.VMEM((4, size, width), BF),
            pltpu.VMEM((4, size, width), BF),
            pltpu.VMEM((2 * size, width), BF),
            pltpu.VMEM((2 * size, width), BF),
            pltpu.VMEM((heads, TILE, 2 * size), BF),
            pltpu.VMEM((2 * size, width), F32),
            pltpu.VMEM((2 * size, width), F32),
        ],
        compiler_params=params(),
        name="backward",
    )(*queries, *grads, *pairs, lse, delta, bias, *([] if dq is None else [dq]))


def spread_kernel(place, dq, dkv, w_ref, o0, o1, o2, o3, rows):
    height = o0.shape[0] // 2
    width = dq.shape[1]

    @pl.when(pl.program_id(0) == 0)
    def _():
        for i in range(8):
            at = pl.ds(pl.multiple_of(place[i] * height, 16), height)
            to = slice(i * height, (i + 1) * height)
            rows[to, :width] = dq[at, :]
            rows[to, width:] = dkv[at, :]

    total = sum(dot_nt(rows[:, c * width : (c + 1) * width], w_ref[c]) for c in range(3)).astype(BF)
    for i, out in enumerate((o0, o1, o2, o3)):
        out[...] = total[2 * i * height : 2 * (i + 1) * height]


def spread(place, dq, dkv, weight, half, chunk=512):
    total, width = dq.shape
    columns = weight.shape[1] // 2
    steps = columns // chunk
    out = jax.ShapeDtypeStruct((total // 4, columns), BF)
    return pl.pallas_call(
        spread_kernel,
        out_shape=(out,) * 4,
        grid_spec=pltpu.PrefetchScalarGridSpec(
            num_scalar_prefetch=1,
            grid=(steps,),
            in_specs=[
                pl.BlockSpec((total, width), lambda k, place: (0, 0)),
                pl.BlockSpec((total, 2 * width), lambda k, place: (0, 0)),
                pl.BlockSpec((3, chunk, width), lambda k, place: (0, k + half * steps, 0)),
            ],
            out_specs=(pl.BlockSpec((total // 4, chunk), lambda k, place: (0, k)),) * 4,
            scratch_shapes=[pltpu.VMEM((total, 3 * width), BF)],
        ),
        compiler_params=params(),
        name="spread",
    )(place, dq, dkv, weight)


def body(hidden_states, qkv_weight, out_grad, tile_frame, frame_band):
    heads = frame_band.shape[0]
    width = qkv_weight.shape[2]
    head_dim = width // heads
    factor = 1.0 / math.sqrt(head_dim)
    scale2 = factor * math.log2(math.e)
    slabs, shards = lax.axis_size("slab"), lax.axis_size("head")
    slab, shard = lax.axis_index("slab"), lax.axis_index("head")
    height, model = hidden_states.shape
    half = model // 2
    slab_tiles = tile_frame.shape[0] // slabs

    def along_y(x, k):
        return lax.ppermute(x, "slab", [(i, (i + 4 * k) % slabs) for i in range(slabs)])

    def across_x(x):
        return lax.ppermute(x, "slab", [(i, i ^ 2) for i in range(slabs)])

    def across_core(x):
        return lax.ppermute(x, "slab", [(i, i ^ 1) for i in range(slabs)])

    def along_z(x, k):
        return lax.ppermute(x, "head", [(i, (i + 2 * k) % shards) for i in range(shards)])

    def across_far(x):
        return lax.ppermute(x, "head", [(i, i ^ 1) for i in range(shards)])

    z, far = shard // 2, shard % 2
    place = jnp.stack([((z + dz) % 4) * 2 + (far ^ dx) for dz in STEPS for dx in (0, 1)]).astype(jnp.int32)

    y, low = slab // 4, slab % 4
    frames = tile_frame.reshape(slabs, slab_tiles)
    query_frames = jnp.stack([frames[((y + d) % 4) * 4 + low] for d in STEPS])
    key_frames = jnp.concatenate([frames[y * 4 + (low ^ d)] for d in (0, 1, 2, 3)])
    distance = jnp.abs(query_frames[:, None, :] - key_frames[None, :, None])
    inside = distance[:, None] <= frame_band[None, :, None, None]
    bias = jnp.repeat(jnp.where(inside, 0.0, -FAR).astype(F32), TILE, axis=3)

    a, b = hidden_states[:, :half], hidden_states[:, half:]
    fa, fb = across_far(a), across_far(b)
    up = [along_z(x, 1) for x in (a, b, fa, fb)]
    down = [along_z(x, -1) for x in (a, b, fa, fb)]
    two_a = [along_z(up[0], 1), along_z(up[2], 1)]
    two_b = [along_z(down[1], -1), along_z(down[3], -1)]
    first = [a, fa, up[0], up[2], down[0], down[2], two_a[0], two_a[1]]
    second = [b, fb, up[1], up[3], down[1], down[3], two_b[0], two_b[1]]
    grads = [out_grad, along_y(out_grad, 1), along_y(out_grad, -1), along_y(out_grad, 2)]

    acc = project(place, first, qkv_weight, 0)
    queries_own, pair_own = project(place, second, qkv_weight, 1, acc)

    queries = [queries_own, along_y(queries_own, 1), along_y(queries_own, -1), along_y(queries_own, 2)]
    pair_x = across_x(pair_own)
    pairs = [pair_own, across_core(pair_own), pair_x, across_core(pair_x)]

    out_t, stat = forward(scale2, queries, grads, pairs, bias)
    stats = [stat, along_y(stat, 1), along_y(stat, -1), along_y(stat, 2)]
    lse, delta = totals(stats)

    def home(blocks):
        return [blocks[0], along_y(blocks[2], 1), along_y(blocks[1], -1), along_y(blocks[3], 2)]

    tiles = 2 * slab_tiles
    dx, dxc, dq = backward(
        scale2, factor, queries, grads, pairs[2:], lse, delta, bias[:, :, tiles:]
    )
    near = across_x(dx + across_core(dxc))
    down_own, down_core, dq = backward(
        scale2, factor, queries, grads, pairs[:2], lse, delta, bias[:, :, :tiles], dq
    )
    attn_out = merge(home(out_t), stats)
    pair_grad = (
        down_own.astype(F32) + across_core(down_core).astype(F32) + near.astype(F32)
    ).astype(BF)
    query_grad = sum(x.astype(F32) for x in home(dq)).astype(BF)

    done = []
    for which in (0, 1):
        own, prev, succ, two = spread(place, query_grad, pair_grad, qkv_weight, which)
        if which == 0:
            succ = succ + along_z(two, 1)
        else:
            prev = prev + along_z(two, -1)
        got = own.astype(F32) + along_z(succ, 1).astype(F32) + along_z(prev, -1).astype(F32)
        other = across_far(got[height:].astype(BF))
        done.append((got[:height] + other.astype(F32)).astype(BF))
    return (attn_out, jnp.concatenate(done, axis=1))


def solution(mesh):
    placed = (P(("slab", "head"), None), P(None, None, "head"), P("slab", "head"), P(), P("head"))
    return jax.shard_map(
        body,
        mesh=mesh,
        in_specs=placed,
        out_specs=(P("slab", "head"), P(("slab", "head"), None)),
        check_vma=False,
    )
```

time: 529 us -> 250 us (0.47)
  waiting for transfers between devices: 350 us -> 70.8 us
  matrix products: 88.6 us -> 0 us
  Pallas kernels: 0 us -> 88.6 us
  starting transfers between devices: 0.6 us -> 70.7 us
  local copies, waits for them, and re-layouts: 58 us -> 11.9 us
  between operations: 13.9 us -> 1.06 us
  other arithmetic: 14.4 us -> 3.93 us
    reduce_scatter x2 -> x0, waiting for transfers between devices: 193 us -> none  [the longest x1 108 us: body(): lax.psum_scatter(key_terms.astype(jnp.bfloat16), 'slab', scatter_dimensio...]
    all_gather x3 -> x0, waiting for transfers between devices: 155 us -> none  [the longest x1 80.8 us: body(): lax.all_gather(hidden_states, 'head', axis=0, tiled=True)]
    pallas_call x0 -> x9, Pallas kernels: none -> 88.6 us  [the longest x2 28.8 us: backward(): pl.pallas_call(functools.partial(backward_kernel, scale2, factor, dq is N...]
    dot_general x58 -> x0, matrix products: 88.6 us -> none  [the longest x8 18.2 us: block_grads(): jnp.einsum('qhd,khd->hqk', grad_part, value_part, preferred_element_type=...]
    ppermute x0 -> x43, waiting for transfers between devices: none -> 70.8 us  [the longest x15 33.7 us: along_y(): lax.ppermute(x, 'slab', [(i, (i + 4 * k) % slabs) for i in range(slabs)])]
    ppermute x0 -> x43, starting transfers between devices: none -> 70.7 us  [the longest x18 33 us: along_z(): lax.ppermute(x, 'head', [(i, (i + 2 * k) % shards) for i in range(shards)])]
    dynamic_slice x33 -> x1, local copies, waits for them, and re-layouts: 34.4 us -> 0.03 us  [body(): query_frames = jnp.stack([frames[(y + d) % 4 * 4 + low] for d in STEPS])]
    dynamic_update_slice x16 -> x0, local copies, waits for them, and re-layouts: 14.2 us -> none  [backward_block(): key_terms = lax.dynamic_update_slice_in_dim(key_terms, key_block, start, 0)]
  transfers between devices with their start and end apart: 5 -> 43, of which waited for: 5 -> 22; matrix products, arithmetic and copies ran while one was open for 1% -> 4% of each run, Pallas kernels for 0% -> 15%
where the time goes in v1:
time: 250 us; the launch traced here: 247 us
  Pallas kernels  88.6 us (35%)
  waiting for transfers between devices  70.8 us (28%)
  starting transfers between devices  70.7 us (28%)
  local copies, waits for them, and re-layouts  11.9 us (5%)
  other arithmetic  3.93 us (2%)
    ppermute x15, waiting for transfers between devices, along_y(): lax.ppermute(x, 'slab', [(i, (i + 4 * k) % slabs) for i in range(slabs)])  33.7 us
    ppermute x18, starting transfers between devices, along_z(): lax.ppermute(x, 'head', [(i, (i + 2 * k) % shards) for i in range(shards)])  33 us
    pallas_call x2, Pallas kernels, backward(): pl.pallas_call(functools.partial(backward_kernel, scale2, factor, dq is N...  28.8 us
    ppermute x18, waiting for transfers between devices, along_z(): lax.ppermute(x, 'head', [(i, (i + 2 * k) % shards) for i in range(shards)])  27.6 us
    ppermute x15, starting transfers between devices, along_y(): lax.ppermute(x, 'slab', [(i, (i + 4 * k) % slabs) for i in range(slabs)])  24.6 us
    pallas_call x2, Pallas kernels, project(): pl.pallas_call(body, out_shape=out_shape, grid_spec=pltpu.PrefetchScalarG...  20 us
    pallas_call x2, Pallas kernels, spread(): pl.pallas_call(spread_kernel, out_shape=(out,) * 4, grid_spec=pltpu.Prefe...  18.3 us
    pallas_call x1, Pallas kernels, forward(): pl.pallas_call(functools.partial(forward_kernel, scale2), out_shape=(jax....  17.2 us
  transfers between devices with their start and end apart: 43, of which 22 were waited for; matrix products, arithmetic and copies ran while one was open for 4% of the time, Pallas kernels for 15%

profile of v1, /device:TPU:0, one launch (start us, length us, event | category | flops | bytes accessed | tf_op | source)
XLA Modules:
  0.0 247.0 jit_solution(12436299359860083994)
XLA Ops:
  0.6 1.1 fusion.9
  1.7 3.2 %collective-permute-start.7 = (bf16[48,3072]{1,0:T(8,128)(2,1)S(1)}, bf16[48,3072]{1,0:T(8,128)(2,1)S(1)}, u32[]{:S(2)}, u32[]{:S(2)}) collective-permute-start(bf16[48,3072]{1,0:T(8,128)(2,1)S(1)} %get-tuple-element.49.refs_0_), channel_id=1, source_target_pairs={{0,1},{1,0},{2,3},{3,2},{4,5},{5,4},{6,7},{7,6},{8,9},{9,8},{10,11... | collective-permute-start | bytes 884744 | tf_op jit(solution)/shard_map/ppermute | solution.py:349
  4.9 1.9 collective-permute-start.8
  6.9 2.1 collective-permute-start.10
  9.5 2.0 collective-permute-start.3
  11.5 0.8 collective-permute-done.7.refs_1_
  12.3 2.9 %collective-permute-start.9 = (bf16[48,3072]{1,0:T(8,128)(2,1)S(1)}, bf16[48,3072]{1,0:T(8,128)(2,1)S(1)}, u32[]{:S(2)}, u32[]{:S(2)}) collective-permute-start(bf16[48,3072]{1,0:T(8,128)(2,1)S(1)} %collective-permute-done.7.refs_1_), channel_id=1, source_target_pairs={{0,2},{1,3},{2,4},{3,5},{4,6},{5,7},{6,0},{7,1},{8,10},{9,11},{10,... | collective-permute-start | bytes 884744 | tf_op jit(solution)/shard_map/ppermute | solution.py:346
  15.7 1.5 collective-permute-start.12
  17.2 3.0 %collective-permute-start.11 = (bf16[48,3072]{1,0:T(8,128)(2,1)S(1)}, bf16[48,3072]{1,0:T(8,128)(2,1)S(1)}, u32[]{:S(2)}, u32[]{:S(2)}) collective-permute-start(bf16[48,3072]{1,0:T(8,128)(2,1)S(1)} %collective-permute-done.7.refs_1_), channel_id=1, source_target_pairs={{0,6},{1,7},{2,0},{3,1},{4,2},{5,3},{6,4},{7,5},{8,14},{9,15},{10,... | collective-permute-start | bytes 884744 | tf_op jit(solution)/shard_map/ppermute | solution.py:346
  20.1 2.4 collective-permute-start.4
  23.1 1.9 collective-permute-start.1
  25.3 1.4 collective-permute-start.13
  26.7 4.9 %collective-permute-done.12.refs_6_ = bf16[48,3072]{1,0:T(8,128)(2,1)S(1)} collective-permute-done((bf16[48,3072]{1,0:T(8,128)(2,1)S(1)}, bf16[48,3072]{1,0:T(8,128)(2,1)S(1)}, u32[]{:S(2)}, u32[]{:S(2)}) %collective-permute-start.12) | collective-permute-done | bytes 294944 | tf_op jit(solution)/shard_map/ppermute | solution.py:346
  31.6 3.2 %collective-permute-start.5 = (bf16[48,3072]{1,0:T(8,128)(2,1)S(1)}, bf16[48,3072]{1,0:T(8,128)(2,1)}, u32[]{:S(2)}, u32[]{:S(2)}) collective-permute-start(bf16[48,3072]{1,0:T(8,128)(2,1)S(1)} %collective-permute-done.3.refs_4_), channel_id=1, source_target_pairs={{0,6},{1,7},{2,0},{3,1},{4,2},{5,3},{6,4},{7,5},{8,14},{9,15},{10,... | collective-permute-start | bytes 884744 | tf_op jit(solution)/shard_map/ppermute | solution.py:346
  34.8 0.9 collective-permute-done.4.refs_5_
  35.8 3.3 %collective-permute-start.6 = (bf16[48,3072]{1,0:T(8,128)(2,1)S(1)}, bf16[48,3072]{1,0:T(8,128)(2,1)}, u32[]{:S(2)}, u32[]{:S(2)}) collective-permute-start(bf16[48,3072]{1,0:T(8,128)(2,1)S(1)} %collective-permute-done.4.refs_5_), channel_id=1, source_target_pairs={{0,6},{1,7},{2,0},{3,1},{4,2},{5,3},{6,4},{7,5},{8,14},{9,15},{10,... | collective-permute-start | bytes 884744 | tf_op jit(solution)/shard_map/ppermute | solution.py:346
  39.7 4.6 %collective-permute-done.13.refs_7_ = bf16[48,3072]{1,0:T(8,128)(2,1)} collective-permute-done((bf16[48,3072]{1,0:T(8,128)(2,1)S(1)}, bf16[48,3072]{1,0:T(8,128)(2,1)}, u32[]{:S(2)}, u32[]{:S(2)}) %collective-permute-start.13) | collective-permute-done | bytes 294944 | tf_op jit(solution)/shard_map/ppermute | solution.py:346
  44.4 9.9 %project.2.refs_9_ = f32[3,384,384]{2,1,0:T(8,128)} custom-call(s32[8]{0:T(128)} %stack.38.place, bf16[48,3072]{1,0:T(8,128)(2,1)} %copy-done.14, bf16[48,3072]{1,0:T(8,128)(2,1)} %copy-done.29, bf16[48,3072]{1,0:T(8,128)(2,1)} %copy-done.30, bf16[48,3072]{1,0:T(8,128)(2,1)} %copy-done.33, bf16[48,3072]{1,0:T(8,128)(2,1)} %copy-done.31, ...), custom_call_target="tpu_custom_call" | custom-call | tf_op jit(solution)/shard_map/project/pallas_call | solution.py:85
  55.0 10.2 %project.3 = (bf16[384,384]{1,0:T(8,128)(2,1)}, bf16[384,768]{1,0:T(8,128)(2,1)}) custom-call(s32[8]{0:T(128)} %stack.38.place, bf16[48,3072]{1,0:T(8,128)(2,1)} %copy-done.13, bf16[48,3072]{1,0:T(8,128)(2,1)} %copy-done.27, bf16[48,3072]{1,0:T(8,128)(2,1)} %copy-done.34, bf16[48,3072]{1,0:T(8,128)(2,1)} %collective-permute-done.2.refs_3_, ...), custom_call_target="tpu_custom_call" | custom-call | tf_op jit(solution)/shard_map/project/pallas_call | solution.py:85
  65.2 1.5 collective-permute-start.21
  66.7 3.2 %collective-permute-start.19 = (bf16[384,384]{1,0:T(8,128)(2,1)S(1)}, bf16[384,384]{1,0:T(8,128)(2,1)S(1)}, u32[]{:S(2)}, u32[]{:S(2)}) collective-permute-start(bf16[384,384]{1,0:T(8,128)(2,1)S(1)} %copy-done), channel_id=1, source_target_pairs={{0,64},{8,72},{16,80},{24,88},{32,96},{40,104},{48,112},{56,120},{... | collective-permute-start | bytes 884744 | tf_op jit(solution)/shard_map/ppermute | solution.py:337
  69.9 1.1 collective-permute-start.18
  70.9 1.0 collective-permute-start.17
  72.1 3.2 %collective-permute-done.21.kv2.refs_8_ = bf16[384,768]{1,0:T(8,128)(2,1)S(1)} collective-permute-done((bf16[384,768]{1,0:T(8,128)(2,1)}, bf16[384,768]{1,0:T(8,128)(2,1)S(1)}, u32[]{:S(2)}, u32[]{:S(2)}) %collective-permute-start.21) | collective-permute-done | bytes 589856 | tf_op jit(solution)/shard_map/ppermute | solution.py:340
  75.4 3.3 %collective-permute-start.16 = (bf16[384,384]{1,0:T(8,128)(2,1)}, bf16[384,384]{1,0:T(8,128)(2,1)S(1)}, u32[]{:S(2)}, u32[]{:S(2)}) collective-permute-start(bf16[384,384]{1,0:T(8,128)(2,1)} %get-tuple-element.22.q0.refs_0_), channel_id=1, source_target_pairs={{0,64},{8,72},{16,80},{24,88},{32,96},{40,104},{48,112},{56,120},{... | collective-permute-start | bytes 884744 | tf_op jit(solution)/shard_map/ppermute | solution.py:337
  78.7 2.4 collective-permute-start.15
  81.3 0.9 broadcast_in_dim.17
  82.2 1.8 reshape.18
  84.0 1.7 copy.7.bias
  85.7 1.3 collective-permute-done.16.q3.refs_3_
  87.1 6.3 %collective-permute-done.15.q2.refs_2_ = bf16[384,384]{1,0:T(8,128)(2,1)S(1)} collective-permute-done((bf16[384,384]{1,0:T(8,128)(2,1)}, bf16[384,384]{1,0:T(8,128)(2,1)S(1)}, u32[]{:S(2)}, u32[]{:S(2)}) %collective-permute-start.15) | collective-permute-done | bytes 294944 | tf_op jit(solution)/shard_map/ppermute | solution.py:337
  95.2 17.2 %forward.1 = (bf16[4,3,128,384]{3,2,1,0:T(8,128)(2,1)}, f32[4,9,384]{2,1,0:T(8,128)}) custom-call(bf16[384,384]{1,0:T(8,128)(2,1)} %get-tuple-element.22.q0.refs_0_, bf16[384,384]{1,0:T(8,128)(2,1)} %copy-done.6, bf16[384,384]{1,0:T(8,128)(2,1)} %copy-done.5, bf16[384,384]{1,0:T(8,128)(2,1)} %copy-done.4, bf16[384,384]{1,0:T(8,128)(2,1)} %refs_4_.3, ...), custom_call_target="tpu_custom_call" | custom-call | tf_op jit(solution)/shard_map/forward/pallas_call | solution.py:141
  112.4 2.7 %collective-permute-start.28 = (f32[4,9,384]{2,1,0:T(8,128)}, f32[4,9,384]{2,1,0:T(8,128)S(1)}, u32[]{:S(2)}, u32[]{:S(2)}) collective-permute-start(f32[4,9,384]{2,1,0:T(8,128)} %get-tuple-element.25.s0), channel_id=1, source_target_pairs={{0,64},{8,72},{16,80},{24,88},{32,96},{40,104},{48,112},{56,120},{... | collective-permute-start | bytes 165896 | tf_op jit(solution)/shard_map/ppermute | solution.py:337
  115.1 1.2 collective-permute-start.27
  117.9 1.1 collective-permute-done.28.s3
  119.0 1.9 collective-permute-done.27.s2
  120.9 1.5 collective-permute-done.26.s1
  123.0 1.7 totals.1
  124.7 14.0 %backward.2 = (bf16[384,768]{1,0:T(8,128)(2,1)}, bf16[384,768]{1,0:T(8,128)(2,1)}, f32[4,3,128,384]{3,2,1,0:T(8,128)}) custom-call(bf16[384,384]{1,0:T(8,128)(2,1)} %get-tuple-element.22.q0.refs_0_, bf16[384,384]{1,0:T(8,128)(2,1)} %copy-done.6, bf16[384,384]{1,0:T(8,128)(2,1)} %copy-done.5, bf16[384,384]{1,0:T(8,128)(2,1)} %copy-done.4, ...), custom_call_target="tpu_custom_call" | custom-call | tf_op jit(solution)/shard_map/backward/pallas_call | solution.py:266
  138.7 14.9 %backward.3 = (bf16[384,768]{1,0:T(8,128)(2,1)}, bf16[384,768]{1,0:T(8,128)(2,1)}, bf16[4,384,384]{2,1,0:T(8,128)(2,1)}) custom-call(bf16[384,384]{1,0:T(8,128)(2,1)} %get-tuple-element.22.q0.refs_0_, bf16[384,384]{1,0:T(8,128)(2,1)} %copy-done.6, bf16[384,384]{1,0:T(8,128)(2,1)} %copy-done.5, bf16[384,384]{1,0:T(8,128)(2,1)} %copy-done.4, ...), custom_call_target="tpu_custom_call" | custom-call | tf_op jit(solution)/shard_map/backward/pallas_call | solution.py:266
  154.3 1.6 collective-permute-start.34
  156.5 2.9 %collective-permute-start.31 = (bf16[384,384]{1,0:T(8,128)(2,1)S(1)}, bf16[384,384]{1,0:T(8,128)(2,1)S(1)}, u32[]{:S(2)}, u32[]{:S(2)}) collective-permute-start(bf16[384,384]{1,0:T(8,128)(2,1)S(1)} %get-tuple-element.43), channel_id=1, source_target_pairs={{0,64},{8,72},{16,80},{24,88},{32,96},{40,104},{48,112},{56,120},{... | collective-permute-start | bytes 884744 | tf_op jit(solution)/shard_map/ppermute | solution.py:337
  160.0 7.1 %collective-permute-done.29 = bf16[384,384]{1,0:T(8,128)(2,1)S(1)} collective-permute-done((bf16[384,384]{1,0:T(8,128)(2,1)S(1)}, bf16[384,384]{1,0:T(8,128)(2,1)S(1)}, u32[]{:S(2)}, u32[]{:S(2)}) %collective-permute-start.29) | collective-permute-done | bytes 294944 | tf_op jit(solution)/shard_map/ppermute | solution.py:337
  167.1 5.2 %collective-permute-done.31 = bf16[384,384]{1,0:T(8,128)(2,1)S(1)} collective-permute-done((bf16[384,384]{1,0:T(8,128)(2,1)S(1)}, bf16[384,384]{1,0:T(8,128)(2,1)S(1)}, u32[]{:S(2)}, u32[]{:S(2)}) %collective-permute-start.31) | collective-permute-done | bytes 294944 | tf_op jit(solution)/shard_map/ppermute | solution.py:337
  172.9 0.9 fusion.4.dq
  173.8 1.0 add_convert_fusion.dkv
  174.8 9.3 %spread.3 = (bf16[96,3072]{1,0:T(8,128)(2,1)}, bf16[96,3072]{1,0:T(8,128)(2,1)}, bf16[96,3072]{1,0:T(8,128)(2,1)}, bf16[96,3072]{1,0:T(8,128)(2,1)}) custom-call(s32[8]{0:T(128)} %stack.38.place, bf16[384,384]{1,0:T(8,128)(2,1)} %fusion.4.dq, bf16[384,768]{1,0:T(8,128)(2,1)} %add_convert_fusion.dkv, bf16[3,6144,384]{2,1,0:T(8,128)(2,1)} %w_ref.3), custom_call_target="tpu_custom_call" | custom-call | tf_op jit(solution)/shard_map/spread/pallas_call | solution.py:305
  184.0 2.0 collective-permute-start.40
  186.0 0.8 slice_bitcast_fusion.3
  186.9 1.3 collective-permute-start.25
  188.2 9.1 %spread.2 = (bf16[96,3072]{1,0:T(8,128)(2,1)}, bf16[96,3072]{1,0:T(8,128)(2,1)}, bf16[96,3072]{1,0:T(8,128)(2,1)}, bf16[96,3072]{1,0:T(8,128)(2,1)}) custom-call(s32[8]{0:T(128)} %stack.38.place, bf16[384,384]{1,0:T(8,128)(2,1)} %fusion.4.dq, bf16[384,768]{1,0:T(8,128)(2,1)} %add_convert_fusion.dkv, bf16[3,6144,384]{2,1,0:T(8,128)(2,1)} %w_ref.3), custom_call_target="tpu_custom_call" | custom-call | tf_op jit(solution)/shard_map/spread/pallas_call | solution.py:305
  197.4 1.1 collective-permute-done.40
  198.6 3.2 %collective-permute-start.41 = (bf16[96,3072]{1,0:T(8,128)(2,1)S(1)}, bf16[96,3072]{1,0:T(8,128)(2,1)S(1)}, u32[]{:S(2)}, u32[]{:S(2)}) collective-permute-start(bf16[96,3072]{1,0:T(8,128)(2,1)S(1)} %add.223), channel_id=1, source_target_pairs={{0,6},{1,7},{2,0},{3,1},{4,2},{5,3},{6,4},{7,5},{8,14},{9,15},{10,... | collective-permute-start | bytes 1769480 | tf_op jit(solution)/shard_map/ppermute | solution.py:346
  201.9 3.7 %collective-permute-start.24 = (bf16[3,128,384]{2,1,0:T(8,128)(2,1)S(1)}, bf16[3,128,384]{2,1,0:T(8,128)(2,1)S(1)}, u32[]{:S(2)}, u32[]{:S(2)}) collective-permute-start(bf16[3,128,384]{2,1,0:T(8,128)(2,1)S(1)} %get-tuple-element.46), channel_id=1, source_target_pairs={{0,96},{8,104},{16,112},{24,120},{32,0},{40,8},{48,16},{56,24},{64... | collective-permute-start | bytes 884744 | tf_op jit(solution)/shard_map/ppermute | solution.py:337
  205.6 5.3 %collective-permute-done.24.o2 = bf16[3,128,384]{2,1,0:T(8,128)(2,1)S(1)} collective-permute-done((bf16[3,128,384]{2,1,0:T(8,128)(2,1)S(1)}, bf16[3,128,384]{2,1,0:T(8,128)(2,1)S(1)}, u32[]{:S(2)}, u32[]{:S(2)}) %collective-permute-start.24) | collective-permute-done | bytes 294944 | tf_op jit(solution)/shard_map/ppermute | solution.py:337
  210.9 3.4 %collective-permute-done.23.o1 = bf16[3,128,384]{2,1,0:T(8,128)(2,1)S(1)} collective-permute-done((bf16[3,128,384]{2,1,0:T(8,128)(2,1)S(1)}, bf16[3,128,384]{2,1,0:T(8,128)(2,1)S(1)}, u32[]{:S(2)}, u32[]{:S(2)}) %collective-permute-start.23) | collective-permute-done | bytes 294944 | tf_op jit(solution)/shard_map/ppermute | solution.py:337
  215.0 2.4 merge.1
  217.9 1.7 collective-permute-start.36
  219.7 7.9 %collective-permute-done.39 = bf16[96,3072]{1,0:T(8,128)(2,1)S(1)} collective-permute-done((bf16[96,3072]{1,0:T(8,128)(2,1)}, bf16[96,3072]{1,0:T(8,128)(2,1)S(1)}, u32[]{:S(2)}, u32[]{:S(2)}) %collective-permute-start.39) | collective-permute-done | bytes 589856 | tf_op jit(solution)/shard_map/ppermute | solution.py:346
  227.8 2.8 %collective-permute-start.42 = (bf16[48,3072]{1,0:T(8,128)(2,1)S(1)}, bf16[48,3072]{1,0:T(8,128)(2,1)S(1)}, u32[]{:S(2)}, u32[]{:S(2)}) collective-permute-start(bf16[48,3072]{1,0:T(8,128)(2,1)S(1)} %slice.88), channel_id=1, source_target_pairs={{0,1},{1,0},{2,3},{3,2},{4,5},{5,4},{6,7},{7,6},{8,9},{9,8},{10,11... | collective-permute-start | bytes 884744 | tf_op jit(solution)/shard_map/ppermute | solution.py:349
  230.6 6.9 %collective-permute-done.36 = bf16[96,3072]{1,0:T(8,128)(2,1)S(1)} collective-permute-done((bf16[96,3072]{1,0:T(8,128)(2,1)S(1)}, bf16[96,3072]{1,0:T(8,128)(2,1)S(1)}, u32[]{:S(2)}, u32[]{:S(2)}) %collective-permute-start.36) | collective-permute-done | bytes 589856 | tf_op jit(solution)/shard_map/ppermute | solution.py:346
  237.8 2.8 %collective-permute-start.38 = (bf16[48,3072]{1,0:T(8,128)(2,1)S(1)}, bf16[48,3072]{1,0:T(8,128)(2,1)S(1)}, u32[]{:S(2)}, u32[]{:S(2)}) collective-permute-start(bf16[48,3072]{1,0:T(8,128)(2,1)S(1)} %slice.89), channel_id=1, source_target_pairs={{0,1},{1,0},{2,3},{3,2},{4,5},{5,4},{6,7},{7,6},{8,9},{9,8},{10,11... | collective-permute-start | bytes 884744 | tf_op jit(solution)/shard_map/ppermute | solution.py:349
  240.7 5.4 %collective-permute-done.38 = bf16[48,3072]{1,0:T(8,128)(2,1)S(1)} collective-permute-done((bf16[48,3072]{1,0:T(8,128)(2,1)S(1)}, bf16[48,3072]{1,0:T(8,128)(2,1)S(1)}, u32[]{:S(2)}, u32[]{:S(2)}) %collective-permute-start.38) | collective-permute-done | bytes 294944 | tf_op jit(solution)/shard_map/ppermute | solution.py:349
  246.2 0.9 pad_maximum_fusion
  (135 shorter events, 12.2 us)
Async XLA Ops:
  1.7 42.6 %copy-start.14 = (bf16[48,3072]{1,0:T(8,128)(2,1)}, bf16[48,3072]{1,0:T(8,128)(2,1)S(1)}, u32[]{:S(2)}) copy-start(bf16[48,3072]{1,0:T(8,128)(2,1)S(1)} %get-tuple-element.49.refs_0_) | copy-start | bytes 884740
  1.7 52.5 %copy-start.13 = (bf16[48,3072]{1,0:T(8,128)(2,1)}, bf16[48,3072]{1,0:T(8,128)(2,1)S(1)}, u32[]{:S(2)}) copy-start(bf16[48,3072]{1,0:T(8,128)(2,1)S(1)} %get-tuple-element.50.refs_0_) | copy-start | bytes 884740
  1.7 10.6 %collective-permute-start.7 = (bf16[48,3072]{1,0:T(8,128)(2,1)S(1)}, bf16[48,3072]{1,0:T(8,128)(2,1)S(1)}, u32[]{:S(2)}, u32[]{:S(2)}) collective-permute-start(bf16[48,3072]{1,0:T(8,128)(2,1)S(1)} %get-tuple-element.49.refs_0_), channel_id=1, source_target_pairs={{0,1},{1,0},{2,3},{3,2},{4,5},{5,4},{6,7},{7,6},{8,9},{9,8},{10,11... | collective-permute-start | bytes 884744 | tf_op jit(solution)/shard_map/ppermute | solution.py:349
  4.9 10.8 %collective-permute-start.8 = (bf16[48,3072]{1,0:T(8,128)(2,1)S(1)}, bf16[48,3072]{1,0:T(8,128)(2,1)S(1)}, u32[]{:S(2)}, u32[]{:S(2)}) collective-permute-start(bf16[48,3072]{1,0:T(8,128)(2,1)S(1)} %get-tuple-element.49.refs_0_), channel_id=1, source_target_pairs={{0,2},{1,3},{2,4},{3,5},{4,6},{5,7},{6,0},{7,1},{8,10},{9,11},{10,... | collective-permute-start | bytes 884744 | tf_op jit(solution)/shard_map/ppermute | solution.py:346
  6.9 10.3 %collective-permute-start.10 = (bf16[48,3072]{1,0:T(8,128)(2,1)S(1)}, bf16[48,3072]{1,0:T(8,128)(2,1)S(1)}, u32[]{:S(2)}, u32[]{:S(2)}) collective-permute-start(bf16[48,3072]{1,0:T(8,128)(2,1)S(1)} %get-tuple-element.49.refs_0_), channel_id=1, source_target_pairs={{0,6},{1,7},{2,0},{3,1},{4,2},{5,3},{6,4},{7,5},{8,14},{9,15},{10,... | collective-permute-start | bytes 884744 | tf_op jit(solution)/shard_map/ppermute | solution.py:346
  9.0 11.1 %collective-permute-start = (bf16[48,3072]{1,0:T(8,128)(2,1)S(1)}, bf16[48,3072]{1,0:T(8,128)(2,1)S(1)}, u32[]{:S(2)}, u32[]{:S(2)}) collective-permute-start(bf16[48,3072]{1,0:T(8,128)(2,1)S(1)} %get-tuple-element.50.refs_0_), channel_id=1, source_target_pairs={{0,1},{1,0},{2,3},{3,2},{4,5},{5,4},{6,7},{7,6},{8,9},{9,8},{10,11... | collective-permute-start | bytes 884744 | tf_op jit(solution)/shard_map/ppermute | solution.py:349
  9.5 13.6 %collective-permute-start.3 = (bf16[48,3072]{1,0:T(8,128)(2,1)S(1)}, bf16[48,3072]{1,0:T(8,128)(2,1)S(1)}, u32[]{:S(2)}, u32[]{:S(2)}) collective-permute-start(bf16[48,3072]{1,0:T(8,128)(2,1)S(1)} %get-tuple-element.50.refs_0_), channel_id=1, source_target_pairs={{0,6},{1,7},{2,0},{3,1},{4,2},{5,3},{6,4},{7,5},{8,14},{9,15},{10,... | collective-permute-start | bytes 884744 | tf_op jit(solution)/shard_map/ppermute | solution.py:346
  12.3 32.0 %copy-start.29 = (bf16[48,3072]{1,0:T(8,128)(2,1)}, bf16[48,3072]{1,0:T(8,128)(2,1)S(1)}, u32[]{:S(2)}) copy-start(bf16[48,3072]{1,0:T(8,128)(2,1)S(1)} %collective-permute-done.7.refs_1_) | copy-start | bytes 884740
  12.3 12.9 %collective-permute-start.9 = (bf16[48,3072]{1,0:T(8,128)(2,1)S(1)}, bf16[48,3072]{1,0:T(8,128)(2,1)S(1)}, u32[]{:S(2)}, u32[]{:S(2)}) collective-permute-start(bf16[48,3072]{1,0:T(8,128)(2,1)S(1)} %collective-permute-done.7.refs_1_), channel_id=1, source_target_pairs={{0,2},{1,3},{2,4},{3,5},{4,6},{5,7},{6,0},{7,1},{8,10},{9,11},{10,... | collective-permute-start | bytes 884744 | tf_op jit(solution)/shard_map/ppermute | solution.py:346
  15.7 28.6 %copy-start.30 = (bf16[48,3072]{1,0:T(8,128)(2,1)}, bf16[48,3072]{1,0:T(8,128)(2,1)S(1)}, u32[]{:S(2)}) copy-start(bf16[48,3072]{1,0:T(8,128)(2,1)S(1)} %collective-permute-done.8.refs_2_) | copy-start | bytes 884740
  15.7 15.9 %collective-permute-start.12 = (bf16[48,3072]{1,0:T(8,128)(2,1)S(1)}, bf16[48,3072]{1,0:T(8,128)(2,1)S(1)}, u32[]{:S(2)}, u32[]{:S(2)}) collective-permute-start(bf16[48,3072]{1,0:T(8,128)(2,1)S(1)} %collective-permute-done.8.refs_2_), channel_id=1, source_target_pairs={{0,2},{1,3},{2,4},{3,5},{4,6},{5,7},{6,0},{7,1},{8,10},{9,11},{10,... | collective-permute-start | bytes 884744 | tf_op jit(solution)/shard_map/ppermute | solution.py:346
  17.2 27.2 %copy-start.31 = (bf16[48,3072]{1,0:T(8,128)(2,1)}, bf16[48,3072]{1,0:T(8,128)(2,1)S(1)}, u32[]{:S(2)}) copy-start(bf16[48,3072]{1,0:T(8,128)(2,1)S(1)} %collective-permute-done.10.refs_4_) | copy-start | bytes 884740
  17.2 14.4 %collective-permute-start.11 = (bf16[48,3072]{1,0:T(8,128)(2,1)S(1)}, bf16[48,3072]{1,0:T(8,128)(2,1)S(1)}, u32[]{:S(2)}, u32[]{:S(2)}) collective-permute-start(bf16[48,3072]{1,0:T(8,128)(2,1)S(1)} %collective-permute-done.7.refs_1_), channel_id=1, source_target_pairs={{0,6},{1,7},{2,0},{3,1},{4,2},{5,3},{6,4},{7,5},{8,14},{9,15},{10,... | collective-permute-start | bytes 884744 | tf_op jit(solution)/shard_map/ppermute | solution.py:346
  20.1 34.1 %copy-start.27 = (bf16[48,3072]{1,0:T(8,128)(2,1)}, bf16[48,3072]{1,0:T(8,128)(2,1)S(1)}, u32[]{:S(2)}) copy-start(bf16[48,3072]{1,0:T(8,128)(2,1)S(1)} %collective-permute-done.refs_1_) | copy-start | bytes 884740
  20.1 15.6 %collective-permute-start.4 = (bf16[48,3072]{1,0:T(8,128)(2,1)S(1)}, bf16[48,3072]{1,0:T(8,128)(2,1)S(1)}, u32[]{:S(2)}, u32[]{:S(2)}) collective-permute-start(bf16[48,3072]{1,0:T(8,128)(2,1)S(1)} %collective-permute-done.refs_1_), channel_id=1, source_target_pairs={{0,6},{1,7},{2,0},{3,1},{4,2},{5,3},{6,4},{7,5},{8,14},{9,15},{10,... | collective-permute-start | bytes 884744 | tf_op jit(solution)/shard_map/ppermute | solution.py:346
  23.1 31.1 %copy-start.28 = (bf16[48,3072]{1,0:T(8,128)(2,1)}, bf16[48,3072]{1,0:T(8,128)(2,1)S(1)}, u32[]{:S(2)}) copy-start(bf16[48,3072]{1,0:T(8,128)(2,1)S(1)} %collective-permute-done.3.refs_4_) | copy-start | bytes 884740
  23.1 31.2 %collective-permute-start.1 = (bf16[48,3072]{1,0:T(8,128)(2,1)S(1)}, bf16[48,3072]{1,0:T(8,128)(2,1)S(1)}, u32[]{:S(2)}, u32[]{:S(2)}) collective-permute-start(bf16[48,3072]{1,0:T(8,128)(2,1)S(1)} %get-tuple-element.50.refs_0_), channel_id=1, source_target_pairs={{0,2},{1,3},{2,4},{3,5},{4,6},{5,7},{6,0},{7,1},{8,10},{9,11},{10,... | collective-permute-start | bytes 884744 | tf_op jit(solution)/shard_map/ppermute | solution.py:346
  25.3 19.1 %copy-start.33 = (bf16[48,3072]{1,0:T(8,128)(2,1)}, bf16[48,3072]{1,0:T(8,128)(2,1)S(1)}, u32[]{:S(2)}) copy-start(bf16[48,3072]{1,0:T(8,128)(2,1)S(1)} %collective-permute-done.9.refs_3_) | copy-start | bytes 884740
  25.3 19.1 %collective-permute-start.13 = (bf16[48,3072]{1,0:T(8,128)(2,1)S(1)}, bf16[48,3072]{1,0:T(8,128)(2,1)}, u32[]{:S(2)}, u32[]{:S(2)}) collective-permute-start(bf16[48,3072]{1,0:T(8,128)(2,1)S(1)} %collective-permute-done.9.refs_3_), channel_id=1, source_target_pairs={{0,2},{1,3},{2,4},{3,5},{4,6},{5,7},{6,0},{7,1},{8,10},{9,11},{10,... | collective-permute-start | bytes 884744 | tf_op jit(solution)/shard_map/ppermute | solution.py:346
  31.6 12.8 %copy-start.35 = (bf16[48,3072]{1,0:T(8,128)(2,1)}, bf16[48,3072]{1,0:T(8,128)(2,1)S(1)}, u32[]{:S(2)}) copy-start(bf16[48,3072]{1,0:T(8,128)(2,1)S(1)} %collective-permute-done.12.refs_6_) | copy-start | bytes 884740
  31.6 22.8 %collective-permute-start.2 = (bf16[48,3072]{1,0:T(8,128)(2,1)S(1)}, bf16[48,3072]{1,0:T(8,128)(2,1)}, u32[]{:S(2)}, u32[]{:S(2)}) collective-permute-start(bf16[48,3072]{1,0:T(8,128)(2,1)S(1)} %collective-permute-done.refs_1_), channel_id=1, source_target_pairs={{0,2},{1,3},{2,4},{3,5},{4,6},{5,7},{6,0},{7,1},{8,10},{9,11},{10,... | collective-permute-start | bytes 884744 | tf_op jit(solution)/shard_map/ppermute | solution.py:346
  31.6 12.8 %copy-start.36 = (bf16[48,3072]{1,0:T(8,128)(2,1)}, bf16[48,3072]{1,0:T(8,128)(2,1)S(1)}, u32[]{:S(2)}) copy-start(bf16[48,3072]{1,0:T(8,128)(2,1)S(1)} %collective-permute-done.11.refs_5_) | copy-start | bytes 884740
  31.6 22.7 %collective-permute-start.5 = (bf16[48,3072]{1,0:T(8,128)(2,1)S(1)}, bf16[48,3072]{1,0:T(8,128)(2,1)}, u32[]{:S(2)}, u32[]{:S(2)}) collective-permute-start(bf16[48,3072]{1,0:T(8,128)(2,1)S(1)} %collective-permute-done.3.refs_4_), channel_id=1, source_target_pairs={{0,6},{1,7},{2,0},{3,1},{4,2},{5,3},{6,4},{7,5},{8,14},{9,15},{10,... | collective-permute-start | bytes 884744 | tf_op jit(solution)/shard_map/ppermute | solution.py:346
  35.8 18.5 %copy-start.32 = (bf16[48,3072]{1,0:T(8,128)(2,1)}, bf16[48,3072]{1,0:T(8,128)(2,1)S(1)}, u32[]{:S(2)}) copy-start(bf16[48,3072]{1,0:T(8,128)(2,1)S(1)} %collective-permute-done.4.refs_5_) | copy-start | bytes 884740
  35.8 18.6 %collective-permute-start.6 = (bf16[48,3072]{1,0:T(8,128)(2,1)S(1)}, bf16[48,3072]{1,0:T(8,128)(2,1)}, u32[]{:S(2)}, u32[]{:S(2)}) collective-permute-start(bf16[48,3072]{1,0:T(8,128)(2,1)S(1)} %collective-permute-done.4.refs_5_), channel_id=1, source_target_pairs={{0,6},{1,7},{2,0},{3,1},{4,2},{5,3},{6,4},{7,5},{8,14},{9,15},{10,... | collective-permute-start | bytes 884744 | tf_op jit(solution)/shard_map/ppermute | solution.py:346
  54.3 12.4 %copy-start = (bf16[384,384]{1,0:T(8,128)(2,1)S(1)}, bf16[384,384]{1,0:T(8,128)(2,1)}, u32[]{:S(2)}) copy-start(bf16[384,384]{1,0:T(8,128)(2,1)} %refs_4_.3) | copy-start | bytes 884740
  54.3 17.6 %copy-start.38 = (s32[48]{0:T(128)S(1)}, s32[48]{0:T(128)}, u32[]{:S(2)}) copy-start(s32[48]{0:T(128)} %param.8) | copy-start | bytes 580
  54.3 26.9 %copy-start.37 = (s32[3]{0:T(128)S(1)}, s32[3]{0:T(128)}, u32[]{:S(2)}) copy-start(s32[3]{0:T(128)} %param.9) | copy-start | bytes 40
  65.2 10.1 %collective-permute-start.21 = (bf16[384,768]{1,0:T(8,128)(2,1)}, bf16[384,768]{1,0:T(8,128)(2,1)S(1)}, u32[]{:S(2)}, u32[]{:S(2)}) collective-permute-start(bf16[384,768]{1,0:T(8,128)(2,1)} %get-tuple-element.23.kv0.refs_8_), channel_id=1, source_target_pairs={{0,16},{8,24},{16,0},{24,8},{32,48},{40,56},{48,32},{56,40},{64,80... | collective-permute-start | bytes 1769480 | tf_op jit(solution)/shard_map/ppermute | solution.py:340
  66.7 8.7 %collective-permute-start.19 = (bf16[384,384]{1,0:T(8,128)(2,1)S(1)}, bf16[384,384]{1,0:T(8,128)(2,1)S(1)}, u32[]{:S(2)}, u32[]{:S(2)}) collective-permute-start(bf16[384,384]{1,0:T(8,128)(2,1)S(1)} %copy-done), channel_id=1, source_target_pairs={{0,64},{8,72},{16,80},{24,88},{32,96},{40,104},{48,112},{56,120},{... | collective-permute-start | bytes 884744 | tf_op jit(solution)/shard_map/ppermute | solution.py:337
  69.9 8.8 %collective-permute-start.18 = (bf16[384,384]{1,0:T(8,128)(2,1)S(1)}, bf16[384,384]{1,0:T(8,128)(2,1)S(1)}, u32[]{:S(2)}, u32[]{:S(2)}) collective-permute-start(bf16[384,384]{1,0:T(8,128)(2,1)S(1)} %copy-done), channel_id=1, source_target_pairs={{0,96},{8,104},{16,112},{24,120},{32,0},{40,8},{48,16},{56,24},{64... | collective-permute-start | bytes 884744 | tf_op jit(solution)/shard_map/ppermute | solution.py:337
  70.9 10.2 %collective-permute-start.17 = (bf16[384,384]{1,0:T(8,128)(2,1)S(1)}, bf16[384,384]{1,0:T(8,128)(2,1)S(1)}, u32[]{:S(2)}, u32[]{:S(2)}) collective-permute-start(bf16[384,384]{1,0:T(8,128)(2,1)S(1)} %copy-done), channel_id=1, source_target_pairs={{0,32},{8,40},{16,48},{24,56},{32,64},{40,72},{48,80},{56,88},{64,... | collective-permute-start | bytes 884744 | tf_op jit(solution)/shard_map/ppermute | solution.py:337
  72.0 21.3 %collective-permute-start.20 = (bf16[384,768]{1,0:T(8,128)(2,1)}, bf16[384,768]{1,0:T(8,128)(2,1)S(1)}, u32[]{:S(2)}, u32[]{:S(2)}) collective-permute-start(bf16[384,768]{1,0:T(8,128)(2,1)} %get-tuple-element.23.kv0.refs_8_), channel_id=1, source_target_pairs={{0,8},{8,0},{16,24},{24,16},{32,40},{40,32},{48,56},{56,48},{64,72... | collective-permute-start | bytes 1769480 | tf_op jit(solution)/shard_map/ppermute | solution.py:343
  75.3 18.1 %copy-start.9 = (bf16[384,768]{1,0:T(8,128)(2,1)}, bf16[384,768]{1,0:T(8,128)(2,1)S(1)}, u32[]{:S(2)}) copy-start(bf16[384,768]{1,0:T(8,128)(2,1)S(1)} %collective-permute-done.21.kv2.refs_8_) | copy-start | bytes 1769476
  75.3 18.1 %collective-permute-start.22 = (bf16[384,768]{1,0:T(8,128)(2,1)S(1)}, bf16[384,768]{1,0:T(8,128)(2,1)S(1)}, u32[]{:S(2)}, u32[]{:S(2)}) collective-permute-start(bf16[384,768]{1,0:T(8,128)(2,1)S(1)} %collective-permute-done.21.kv2.refs_8_), channel_id=1, source_target_pairs={{0,8},{8,0},{16,24},{24,16},{32,40},{40,32},{48,56},{56,48},{64,72... | collective-permute-start | bytes 1769480 | tf_op jit(solution)/shard_map/ppermute | solution.py:343
  75.4 18.0 %copy-start.1 = (bf16[384,384]{1,0:T(8,128)(2,1)}, bf16[384,384]{1,0:T(8,128)(2,1)S(1)}, u32[]{:S(2)}) copy-start(bf16[384,384]{1,0:T(8,128)(2,1)S(1)} %collective-permute-done.19.g3.refs_7_) | copy-start | bytes 884740
  75.4 11.6 %collective-permute-start.16 = (bf16[384,384]{1,0:T(8,128)(2,1)}, bf16[384,384]{1,0:T(8,128)(2,1)S(1)}, u32[]{:S(2)}, u32[]{:S(2)}) collective-permute-start(bf16[384,384]{1,0:T(8,128)(2,1)} %get-tuple-element.22.q0.refs_0_), channel_id=1, source_target_pairs={{0,64},{8,72},{16,80},{24,88},{32,96},{40,104},{48,112},{56,120},{... | collective-permute-start | bytes 884744 | tf_op jit(solution)/shard_map/ppermute | solution.py:337
  78.7 14.7 %copy-start.2 = (bf16[384,384]{1,0:T(8,128)(2,1)}, bf16[384,384]{1,0:T(8,128)(2,1)S(1)}, u32[]{:S(2)}) copy-start(bf16[384,384]{1,0:T(8,128)(2,1)S(1)} %collective-permute-done.18.g2.refs_6_) | copy-start | bytes 884740
  78.7 14.6 %collective-permute-start.15 = (bf16[384,384]{1,0:T(8,128)(2,1)}, bf16[384,384]{1,0:T(8,128)(2,1)S(1)}, u32[]{:S(2)}, u32[]{:S(2)}) collective-permute-start(bf16[384,384]{1,0:T(8,128)(2,1)} %get-tuple-element.22.q0.refs_0_), channel_id=1, source_target_pairs={{0,96},{8,104},{16,112},{24,120},{32,0},{40,8},{48,16},{56,24},{64... | collective-permute-start | bytes 884744 | tf_op jit(solution)/shard_map/ppermute | solution.py:337
  81.1 12.2 %collective-permute-start.14 = (bf16[384,384]{1,0:T(8,128)(2,1)}, bf16[384,384]{1,0:T(8,128)(2,1)S(1)}, u32[]{:S(2)}, u32[]{:S(2)}) collective-permute-start(bf16[384,384]{1,0:T(8,128)(2,1)} %get-tuple-element.22.q0.refs_0_), channel_id=1, source_target_pairs={{0,32},{8,40},{16,48},{24,56},{32,64},{40,72},{48,80},{56,88},{64,... | collective-permute-start | bytes 884744 | tf_op jit(solution)/shard_map/ppermute | solution.py:337
  85.7 31.5 %copy-start.7 = (f32[4,3,12,384]{3,2,1,0:T(8,128)S(1)}, f32[4,3,12,384]{3,2,1,0:T(8,128)}, u32[]{:S(2)}) copy-start(f32[4,3,12,384]{3,2,1,0:T(8,128)} %copy.7.bias) | copy-start | bytes 663556
  112.4 6.6 %collective-permute-start.28 = (f32[4,9,384]{2,1,0:T(8,128)}, f32[4,9,384]{2,1,0:T(8,128)S(1)}, u32[]{:S(2)}, u32[]{:S(2)}) collective-permute-start(f32[4,9,384]{2,1,0:T(8,128)} %get-tuple-element.25.s0), channel_id=1, source_target_pairs={{0,64},{8,72},{16,80},{24,88},{32,96},{40,104},{48,112},{56,120},{... | collective-permute-start | bytes 165896 | tf_op jit(solution)/shard_map/ppermute | solution.py:337
  115.1 5.8 %collective-permute-start.27 = (f32[4,9,384]{2,1,0:T(8,128)}, f32[4,9,384]{2,1,0:T(8,128)S(1)}, u32[]{:S(2)}, u32[]{:S(2)}) collective-permute-start(f32[4,9,384]{2,1,0:T(8,128)} %get-tuple-element.25.s0), channel_id=1, source_target_pairs={{0,96},{8,104},{16,112},{24,120},{32,0},{40,8},{48,16},{56,24},{64... | collective-permute-start | bytes 165896 | tf_op jit(solution)/shard_map/ppermute | solution.py:337
  116.4 6.0 %collective-permute-start.26 = (f32[4,9,384]{2,1,0:T(8,128)}, f32[4,9,384]{2,1,0:T(8,128)S(1)}, u32[]{:S(2)}, u32[]{:S(2)}) collective-permute-start(f32[4,9,384]{2,1,0:T(8,128)} %get-tuple-element.25.s0), channel_id=1, source_target_pairs={{0,32},{8,40},{16,48},{24,56},{32,64},{40,72},{48,80},{56,88},{64,... | collective-permute-start | bytes 165896 | tf_op jit(solution)/shard_map/ppermute | solution.py:337
  138.7 15.5 %collective-permute-start.33 = (bf16[384,768]{1,0:T(8,128)(2,1)}, bf16[384,768]{1,0:T(8,128)(2,1)S(1)}, u32[]{:S(2)}, u32[]{:S(2)}) collective-permute-start(bf16[384,768]{1,0:T(8,128)(2,1)} %get-tuple-element.33), channel_id=1, source_target_pairs={{0,8},{8,0},{16,24},{24,16},{32,40},{40,32},{48,56},{56,48},{64,72... | collective-permute-start | bytes 1769480 | tf_op jit(solution)/shard_map/ppermute | solution.py:343
  138.7 15.5 %copy-start.17 = (bf16[384,768]{1,0:T(8,128)(2,1)S(1)}, bf16[384,768]{1,0:T(8,128)(2,1)}, u32[]{:S(2)}) copy-start(bf16[384,768]{1,0:T(8,128)(2,1)} %get-tuple-element.32) | copy-start | bytes 1769476
  153.6 20.1 %collective-permute-start.32 = (bf16[384,768]{1,0:T(8,128)(2,1)}, bf16[384,768]{1,0:T(8,128)(2,1)S(1)}, u32[]{:S(2)}, u32[]{:S(2)}) collective-permute-start(bf16[384,768]{1,0:T(8,128)(2,1)} %get-tuple-element.31), channel_id=1, source_target_pairs={{0,8},{8,0},{16,24},{24,16},{32,40},{40,32},{48,56},{56,48},{64,72... | collective-permute-start | bytes 1769480 | tf_op jit(solution)/shard_map/ppermute | solution.py:343
  154.3 19.4 %collective-permute-start.34 = (bf16[384,768]{1,0:T(8,128)(2,1)S(1)}, bf16[384,768]{1,0:T(8,128)(2,1)S(1)}, u32[]{:S(2)}, u32[]{:S(2)}) collective-permute-start(bf16[384,768]{1,0:T(8,128)(2,1)S(1)} %add.216), channel_id=1, source_target_pairs={{0,16},{8,24},{16,0},{24,8},{32,48},{40,56},{48,32},{56,40},{64,80... | collective-permute-start | bytes 1769480 | tf_op jit(solution)/shard_map/ppermute | solution.py:340
  156.0 17.8 %copy-start.20 = (bf16[384,768]{1,0:T(8,128)(2,1)S(1)}, bf16[384,768]{1,0:T(8,128)(2,1)}, u32[]{:S(2)}) copy-start(bf16[384,768]{1,0:T(8,128)(2,1)} %get-tuple-element.30) | copy-start | bytes 1769476
  156.0 11.1 %collective-permute-start.29 = (bf16[384,384]{1,0:T(8,128)(2,1)S(1)}, bf16[384,384]{1,0:T(8,128)(2,1)S(1)}, u32[]{:S(2)}, u32[]{:S(2)}) collective-permute-start(bf16[384,384]{1,0:T(8,128)(2,1)S(1)} %get-tuple-element.42), channel_id=1, source_target_pairs={{0,32},{8,40},{16,48},{24,56},{32,64},{40,72},{48,80},{56,88},{64,... | collective-permute-start | bytes 884744 | tf_op jit(solution)/shard_map/ppermute | solution.py:337
  156.5 15.8 %collective-permute-start.31 = (bf16[384,384]{1,0:T(8,128)(2,1)S(1)}, bf16[384,384]{1,0:T(8,128)(2,1)S(1)}, u32[]{:S(2)}, u32[]{:S(2)}) collective-permute-start(bf16[384,384]{1,0:T(8,128)(2,1)S(1)} %get-tuple-element.43), channel_id=1, source_target_pairs={{0,64},{8,72},{16,80},{24,88},{32,96},{40,104},{48,112},{56,120},{... | collective-permute-start | bytes 884744 | tf_op jit(solution)/shard_map/ppermute | solution.py:337
  159.4 13.5 %collective-permute-start.30 = (bf16[384,384]{1,0:T(8,128)(2,1)S(1)}, bf16[384,384]{1,0:T(8,128)(2,1)S(1)}, u32[]{:S(2)}, u32[]{:S(2)}) collective-permute-start(bf16[384,384]{1,0:T(8,128)(2,1)S(1)} %get-tuple-element.44), channel_id=1, source_target_pairs={{0,96},{8,104},{16,112},{24,120},{32,0},{40,8},{48,16},{56,24},{64... | collective-permute-start | bytes 884744 | tf_op jit(solution)/shard_map/ppermute | solution.py:337
  184.0 14.4 %collective-permute-start.40 = (bf16[96,3072]{1,0:T(8,128)(2,1)}, bf16[96,3072]{1,0:T(8,128)(2,1)S(1)}, u32[]{:S(2)}, u32[]{:S(2)}) collective-permute-start(bf16[96,3072]{1,0:T(8,128)(2,1)} %get-tuple-element.41), channel_id=1, source_target_pairs={{0,6},{1,7},{2,0},{3,1},{4,2},{5,3},{6,4},{7,5},{8,14},{9,15},{10,... | collective-permute-start | bytes 1769480 | tf_op jit(solution)/shard_map/ppermute | solution.py:346
  186.9 18.7 %collective-permute-start.25 = (bf16[3,128,384]{2,1,0:T(8,128)(2,1)S(1)}, bf16[3,128,384]{2,1,0:T(8,128)(2,1)S(1)}, u32[]{:S(2)}, u32[]{:S(2)}) collective-permute-start(bf16[3,128,384]{2,1,0:T(8,128)(2,1)S(1)} %get-tuple-element.45), channel_id=1, source_target_pairs={{0,64},{8,72},{16,80},{24,88},{32,96},{40,104},{48,112},{56,120},{... | collective-permute-start | bytes 884744 | tf_op jit(solution)/shard_map/ppermute | solution.py:337
  197.2 20.6 %collective-permute-start.35 = (bf16[96,3072]{1,0:T(8,128)(2,1)}, bf16[96,3072]{1,0:T(8,128)(2,1)S(1)}, u32[]{:S(2)}, u32[]{:S(2)}) collective-permute-start(bf16[96,3072]{1,0:T(8,128)(2,1)} %get-tuple-element.36), channel_id=1, source_target_pairs={{0,2},{1,3},{2,4},{3,5},{4,6},{5,7},{6,0},{7,1},{8,10},{9,11},{10,... | collective-permute-start | bytes 1769480 | tf_op jit(solution)/shard_map/ppermute | solution.py:346
  197.3 30.3 %collective-permute-start.39 = (bf16[96,3072]{1,0:T(8,128)(2,1)}, bf16[96,3072]{1,0:T(8,128)(2,1)S(1)}, u32[]{:S(2)}, u32[]{:S(2)}) collective-permute-start(bf16[96,3072]{1,0:T(8,128)(2,1)} %get-tuple-element.39), channel_id=1, source_target_pairs={{0,2},{1,3},{2,4},{3,5},{4,6},{5,7},{6,0},{7,1},{8,10},{9,11},{10,... | collective-permute-start | bytes 1769480 | tf_op jit(solution)/shard_map/ppermute | solution.py:346
  198.6 19.2 %copy-start.15 = (bf16[96,3072]{1,0:T(8,128)(2,1)S(1)}, bf16[96,3072]{1,0:T(8,128)(2,1)}, u32[]{:S(2)}) copy-start(bf16[96,3072]{1,0:T(8,128)(2,1)} %get-tuple-element.35) | copy-start | bytes 1769476
  198.6 28.9 %collective-permute-start.41 = (bf16[96,3072]{1,0:T(8,128)(2,1)S(1)}, bf16[96,3072]{1,0:T(8,128)(2,1)S(1)}, u32[]{:S(2)}, u32[]{:S(2)}) collective-permute-start(bf16[96,3072]{1,0:T(8,128)(2,1)S(1)} %add.223), channel_id=1, source_target_pairs={{0,6},{1,7},{2,0},{3,1},{4,2},{5,3},{6,4},{7,5},{8,14},{9,15},{10,... | collective-permute-start | bytes 1769480 | tf_op jit(solution)/shard_map/ppermute | solution.py:346
  201.9 9.0 %collective-permute-start.24 = (bf16[3,128,384]{2,1,0:T(8,128)(2,1)S(1)}, bf16[3,128,384]{2,1,0:T(8,128)(2,1)S(1)}, u32[]{:S(2)}, u32[]{:S(2)}) collective-permute-start(bf16[3,128,384]{2,1,0:T(8,128)(2,1)S(1)} %get-tuple-element.46), channel_id=1, source_target_pairs={{0,96},{8,104},{16,112},{24,120},{32,0},{40,8},{48,16},{56,24},{64... | collective-permute-start | bytes 884744 | tf_op jit(solution)/shard_map/ppermute | solution.py:337
  205.6 8.7 %collective-permute-start.23 = (bf16[3,128,384]{2,1,0:T(8,128)(2,1)S(1)}, bf16[3,128,384]{2,1,0:T(8,128)(2,1)S(1)}, u32[]{:S(2)}, u32[]{:S(2)}) collective-permute-start(bf16[3,128,384]{2,1,0:T(8,128)(2,1)S(1)} %get-tuple-element.47), channel_id=1, source_target_pairs={{0,32},{8,40},{16,48},{24,56},{32,64},{40,72},{48,80},{56,88},{64,... | collective-permute-start | bytes 884744 | tf_op jit(solution)/shard_map/ppermute | solution.py:337
  217.4 13.2 %collective-permute-start.37 = (bf16[96,3072]{1,0:T(8,128)(2,1)}, bf16[96,3072]{1,0:T(8,128)(2,1)S(1)}, u32[]{:S(2)}, u32[]{:S(2)}) collective-permute-start(bf16[96,3072]{1,0:T(8,128)(2,1)} %get-tuple-element.37), channel_id=1, source_target_pairs={{0,6},{1,7},{2,0},{3,1},{4,2},{5,3},{6,4},{7,5},{8,14},{9,15},{10,... | collective-permute-start | bytes 1769480 | tf_op jit(solution)/shard_map/ppermute | solution.py:346
  217.9 19.6 %collective-permute-start.36 = (bf16[96,3072]{1,0:T(8,128)(2,1)S(1)}, bf16[96,3072]{1,0:T(8,128)(2,1)S(1)}, u32[]{:S(2)}, u32[]{:S(2)}) collective-permute-start(bf16[96,3072]{1,0:T(8,128)(2,1)S(1)} %add.218), channel_id=1, source_target_pairs={{0,2},{1,3},{2,4},{3,5},{4,6},{5,7},{6,0},{7,1},{8,10},{9,11},{10,... | collective-permute-start | bytes 1769480 | tf_op jit(solution)/shard_map/ppermute | solution.py:346
  227.8 12.8 %collective-permute-start.42 = (bf16[48,3072]{1,0:T(8,128)(2,1)S(1)}, bf16[48,3072]{1,0:T(8,128)(2,1)S(1)}, u32[]{:S(2)}, u32[]{:S(2)}) collective-permute-start(bf16[48,3072]{1,0:T(8,128)(2,1)S(1)} %slice.88), channel_id=1, source_target_pairs={{0,1},{1,0},{2,3},{3,2},{4,5},{5,4},{6,7},{7,6},{8,9},{9,8},{10,11... | collective-permute-start | bytes 884744 | tf_op jit(solution)/shard_map/ppermute | solution.py:349
  237.8 8.3 %collective-permute-start.38 = (bf16[48,3072]{1,0:T(8,128)(2,1)S(1)}, bf16[48,3072]{1,0:T(8,128)(2,1)S(1)}, u32[]{:S(2)}, u32[]{:S(2)}) collective-permute-start(bf16[48,3072]{1,0:T(8,128)(2,1)S(1)} %slice.89), channel_id=1, source_target_pairs={{0,1},{1,0},{2,3},{3,2},{4,5},{5,4},{6,7},{7,6},{8,9},{9,8},{10,11... | collective-permute-start | bytes 884744 | tf_op jit(solution)/shard_map/ppermute | solution.py:349
  (18 other events, 86.3 us)
